TPU v7x, 32 devices: a whole 2x2x4 slice. The times are simulated.
32 devices in a mesh: seq: 16 (over z, x, core), tensor: 2 (over y).
Axes of the slice: x: 2, y: 2, z: 4, core: 2. Of those that a mesh axis runs over, the one named last changes fastest.
Arguments:
- hidden: bfloat16 [3072, 4096], P('seq', 'tensor'), may hold values from -170 to 170
- depth: int32 [3072], P('seq'), may hold values from 0 to 4, as said below
- norm_gain: float32 [4096], replicated, may hold values from 0.5 to 2
- w_query: bfloat16 [4096, 2048], P('seq', 'tensor'), may hold values from -2.5 to 2.5
- w_key: bfloat16 [4096, 1024], P('seq', 'tensor'), may hold values from -1 to 1
- w_value: bfloat16 [4096, 1024], P('seq', 'tensor'), may hold values from -0.09375 to 0.09375
- w_out: bfloat16 [2048, 4096], P('tensor', 'seq'), may hold values from -0.1875 to 0.1875
Outputs:
- mixed: bfloat16 [3072, 4096], P('seq', 'tensor')
Inputs may be any that keep to these rules, and one draw needn't show every extreme that they name: A token takes part in this step when its depth exceeds 2. In each aligned block of 192 tokens at most 96 take part, and some block holds exactly 96.
All inputs are finite; a program needn't handle non-finite values.
Results may differ from a plain program's by a relative error of at most 0.015.
Values may be sent and summed in bfloat16 or wider, within the bound.
A program may use at most 64 MiB of HBM per device.

v0:
```python
import jax
import jax.numpy as jnp
from jax import lax
from jax.sharding import PartitionSpec as P

HD = 128
STEP = 2
EPSILON = 1e-05
MASKED_SCORE = -1e30


def block_split(total_rows):
    number = -(-total_rows // 512)
    while total_rows % number != 0:
        number = number + 1
    return number


def online_fold(queries, my_index, slot_width):
    query_rows, kv_heads, group_size, head_size = queries.shape
    query_slot = jnp.arange(query_rows, dtype=jnp.int32)

    def update(running, block):
        row_peak, row_total, weighted = running
        key_block, value_block, flag_block, index_block = block
        scores = jnp.einsum(
            "qjgd,kjd->jgqk", queries, key_block, preferred_element_type=jnp.float32
        ) * head_size ** (-0.5)
        source = index_block // slot_width
        within = index_block % slot_width
        earlier = source[None, :] < my_index
        same_dev = (source[None, :] == my_index) & (within[None, :] <= query_slot[:, None])
        visible = (flag_block[None, :] > 0) & (earlier | same_dev)
        scores = jnp.where(visible[None, None], scores, MASKED_SCORE)
        new_peak = jnp.maximum(row_peak, jnp.max(scores, axis=-1))
        rescale = jnp.exp(row_peak - new_peak)
        expons = jnp.exp(scores - new_peak[..., None])
        row_total = row_total * rescale + jnp.sum(expons, axis=-1)
        weighted = weighted * rescale[..., None] + jnp.einsum(
            "jgqk,kjd->jgqd",
            expons.astype(jnp.bfloat16),
            value_block,
            preferred_element_type=jnp.float32,
        )
        return ((new_peak, row_total, weighted), None)

    def absorb(running, arrived, offset):
        key_rows, value_rows, flag_rows = arrived
        arrived_rows = key_rows.shape[0]
        number = block_split(arrived_rows)
        step_rows = arrived_rows // number
        key_position = jnp.arange(arrived_rows, dtype=jnp.int32)
        shaped = (
            key_rows.reshape(number, step_rows, kv_heads, head_size),
            value_rows.reshape(number, step_rows, kv_heads, head_size),
            flag_rows.reshape(number, step_rows),
            key_position.reshape(number, step_rows),
        )
        running, _ = lax.scan(update, running, shaped)
        return running

    start_state = (
        jnp.full((kv_heads, group_size, query_rows), MASKED_SCORE, jnp.float32),
        jnp.zeros((kv_heads, group_size, query_rows), jnp.float32),
        jnp.zeros((kv_heads, group_size, query_rows, head_size), jnp.float32),
    )
    return (absorb, start_state)


def normalized(running):
    row_peak, row_total, weighted = running
    ratio = weighted / row_total[..., None]
    kv_heads, group_size, query_rows, head_size = ratio.shape
    return (
        jnp.transpose(ratio, (2, 0, 1, 3))
        .reshape(query_rows, kv_heads * group_size * head_size)
        .astype(jnp.bfloat16)
    )


def body(hidden, depth, norm_gain, w_query, w_key, w_value, w_out):
    row_count = hidden.shape[0]
    my_index = lax.axis_index("seq")
    gathered = lax.all_gather(hidden, "tensor", axis=1, tiled=True)
    widened = gathered.astype(jnp.float32)
    inverse = lax.rsqrt(jnp.mean(widened * widened, axis=1, keepdims=True) + EPSILON)
    normed = (widened * inverse * norm_gain[None, :]).astype(jnp.bfloat16)
    arrived = (
        lax.all_gather(w_query, "seq", axis=0, tiled=True),
        lax.all_gather(w_key, "seq", axis=0, tiled=True),
        lax.all_gather(w_value, "seq", axis=0, tiled=True),
    )
    query_sum, key_sum, value_sum = tuple(
        (jnp.dot(normed, matrix, preferred_element_type=jnp.float32) for matrix in arrived)
    )
    kv_heads = w_key.shape[1] // HD
    group_size = w_query.shape[1] // w_key.shape[1]
    queries = query_sum.astype(jnp.bfloat16)
    keys_local = key_sum.astype(jnp.bfloat16)
    values_local = value_sum.astype(jnp.bfloat16)
    living = depth > STEP
    absorb, start_state = online_fold(
        queries.reshape(row_count, kv_heads, group_size, HD), my_index, row_count
    )
    running = absorb(
        start_state,
        (
            lax.all_gather(keys_local, "seq", axis=0, tiled=True),
            lax.all_gather(values_local, "seq", axis=0, tiled=True),
            lax.all_gather(living.astype(jnp.bfloat16), "seq", axis=0, tiled=True),
        ),
        jnp.int32(0),
    )
    attended = normalized(running)
    branch_terms = jnp.dot(
        attended,
        lax.all_gather(w_out, "seq", axis=1, tiled=True),
        preferred_element_type=jnp.float32,
    )
    owned = lax.psum_scatter(
        branch_terms.astype(jnp.bfloat16), "tensor", scatter_dimension=1, tiled=True
    ).astype(jnp.float32)
    return jnp.where(living[:, None], owned, 0.0).astype(jnp.bfloat16)


def solution(mesh):
    return jax.shard_map(
        body,
        mesh=mesh,
        in_specs=(
            P("seq", "tensor"),
            P("seq"),
            P(),
            P("seq", "tensor"),
            P("seq", "tensor"),
            P("seq", "tensor"),
            P("tensor", "seq"),
        ),
        out_specs=P("seq", "tensor"),
        check_vma=False,
    )
```

profile of v0, /device:TPU:0, one launch (start us, length us, event | category | flops | bytes accessed | tf_op | source)
XLA Modules:
  0.0 428.1 jit_solution(162654652320524777)
XLA Ops:
  8.8 30.0 %all-gather.8.cloned.1.call-done = bf16[192,4096]{1,0:T(8,128)(2,1)} async-done(((bf16[192,2048]{1,0:T(8,128)(2,1)}), bf16[192,4096]{1,0:T(8,128)(2,1)}) %all-gather.8.cloned.1.call-update) | async-done | bytes 1572880 | tf_op jit(solution)/shard_map/all_gather | solution.py:84
  38.8 1.8 fusion.22
  40.6 50.7 %all-gather.10.cloned.1.call-done = bf16[4096,512]{1,0:T(8,128)(2,1)} async-done(((bf16[256,512]{1,0:T(8,128)(2,1)}), bf16[4096,512]{1,0:T(8,128)(2,1)}) %all-gather.10.cloned.1.call-update) | async-done | bytes 4194320 | tf_op jit(solution)/shard_map/all_gather | solution.py:90
  91.4 4.4 %convolution_convert_fusion.3 = bf16[192,512]{1,0:T(8,128)(2,1)} fusion(bf16[4096,512]{1,0:T(8,128)(2,1)} %all-gather.10.cloned.1.call-done, bf16[192,4096]{1,0:T(8,128)(2,1)} %all-gather.8.cloned.1.call-done, f32[4096]{0:T(1024)} %param.11, f32[192]{0:T(256)S(1)} %add_rsqrt_fusion), kind=kOutput, calls=%fused_computation.44 | convolution fusion | flops 808550400 | bytes 5980928 | tf_op jit(solution)/shard_map/dot_general | solution.py:94
  95.9 46.6 %all-gather.16.cloned.1.call-done = bf16[4096,512]{1,0:T(8,128)(2,1)} async-done(((bf16[256,512]{1,0:T(8,128)(2,1)}), bf16[4096,512]{1,0:T(8,128)(2,1)}) %all-gather.16.cloned.1.call-update) | async-done | bytes 4194320 | tf_op jit(solution)/shard_map/all_gather | solution.py:91
  142.5 3.9 convolution_convert_fusion.2
  149.4 32.5 %all-reduce = bf16[3072]{0:T(1024)(128)(2,1)S(1)} all-reduce(bf16[3072]{0:T(1024)(128)(2,1)S(1)} %dynamic-update-slice), channel_id=1, replica_groups=mesh['seq'=16,'tensor'=2] {'seq'}, use_global_device_ids=true, to_apply=%add | all-reduce | flops 3072 | bytes 12288
  181.9 6.7 %all-gather.12.cloned.1.call-done = bf16[3072,512]{1,0:T(8,128)(2,1)} async-done(((bf16[192,512]{1,0:T(8,128)(2,1)}), bf16[3072,512]{1,0:T(8,128)(2,1)}) %all-gather.12.cloned.1.call-update) | async-done | bytes 3145744 | tf_op jit(solution)/shard_map/all_gather | solution.py:108
  188.7 5.5 %reshape.131 = bf16[6,512,4,128]{3,2,1,0:T(4,128)(2,1)} reshape(bf16[3072,512]{1,0:T(8,128)(2,1)} %all-gather.12.cloned.1.call-done) | data formatting | bytes 6291456 | tf_op jit(solution)/shard_map/reshape | solution.py:54
  194.2 40.7 %all-gather.18.cloned.1.call-done = bf16[3072,512]{1,0:T(8,128)(2,1)} async-done(((bf16[192,512]{1,0:T(8,128)(2,1)}), bf16[3072,512]{1,0:T(8,128)(2,1)}) %all-gather.18.cloned.1.call-update) | async-done | bytes 3145744 | tf_op jit(solution)/shard_map/all_gather | solution.py:109
  235.0 5.5 %reshape.133 = bf16[6,512,4,128]{3,2,1,0:T(4,128)(2,1)} reshape(bf16[3072,512]{1,0:T(8,128)(2,1)} %all-gather.18.cloned.1.call-done) | data formatting | bytes 6291456 | tf_op jit(solution)/shard_map/reshape | solution.py:55
  240.5 69.2 %all-gather.14.cloned.1.call-done = bf16[4096,1024]{1,0:T(8,128)(2,1)} async-done(((bf16[256,1024]{1,0:T(8,128)(2,1)}), bf16[4096,1024]{1,0:T(8,128)(2,1)}) %all-gather.14.cloned.1.call-update) | async-done | bytes 8388624 | tf_op jit(solution)/shard_map/all_gather | solution.py:89
  309.6 5.2 %convolution_convert_fusion.1 = bf16[192,1024]{1,0:T(8,128)(2,1)S(1)} fusion(bf16[4096,1024]{1,0:T(8,128)(2,1)} %all-gather.14.cloned.1.call-done, bf16[192,4096]{1,0:T(8,128)(2,1)S(1)} %copy-done.1, f32[4096]{0:T(1024)S(1)} %copy-done.5, f32[192]{0:T(256)S(1)} %add_rsqrt_fusion), kind=kOutput, calls=%fused_computation.42 | convolution fusion | flops 1613955072 | bytes 10371840 | tf_op jit(solution)/shard_map/dot_general | solution.py:94
  316.0 46.5 %while.17 = (s32[]{:T(128)}, f32[4,2,192]{2,1,0:T(2,128)S(1)}, f32[4,2,192]{2,1,0:T(2,128)S(1)}, f32[4,2,192,128]{3,2,1,0:T(8,128)}, bf16[6,512]{1,0:T(8,128)(2,...) while((s32[]{:T(128)}, f32[4,2,192]{2,1,0:T(2,128)S(1)}, ...), condition=%wide.region_4.5_spmd.clone, body=%wide.region_1.4_spmd.clone.sunk | while | flops 412303360 | bytes 23443692 | solution.py:59
  316.1 2.4 constant_dynamic-slice_fusion.4
  318.6 1.8 fusion.47
  321.6 1.2 fusion.51
  323.9 2.4 constant_dynamic-slice_fusion.4
  326.3 1.8 fusion.47
  331.6 2.4 constant_dynamic-slice_fusion.4
  334.0 1.8 fusion.47
  339.4 2.4 constant_dynamic-slice_fusion.4
  341.7 1.8 fusion.47
  347.1 2.4 constant_dynamic-slice_fusion.4
  349.5 1.8 fusion.47
  354.8 2.5 constant_dynamic-slice_fusion.4
  357.3 1.8 fusion.47
  362.5 1.4 fusion.25
  364.6 23.6 %all-gather.20.cloned.1.call-done = bf16[1024,4096]{1,0:T(8,128)(2,1)} async-done(((bf16[1024,256]{1,0:T(8,128)(2,1)}), bf16[1024,4096]{1,0:T(8,128)(2,1)}) %all-gather.20.cloned.1.call-update) | async-done | bytes 8388624 | tf_op jit(solution)/shard_map/all_gather | solution.py:117
  388.1 6.4 %convolution_convert_fusion = bf16[192,4096]{1,0:T(8,128)(2,1)} fusion(bf16[192,1024]{1,0:T(8,128)(2,1)S(1)} %convert_element_type.50, bf16[1024,4096]{1,0:T(8,128)(2,1)} %all-gather.20.cloned.1.call-done), kind=kOutput, calls=%fused_computation.35 | convolution fusion | flops 1611399168 | bytes 10354688 | tf_op jit(solution)/shard_map/dot_general | solution.py:115
  394.5 24.5 %reduce-scatter.2.cloned.1.call-done = bf16[192,2048]{1,0:T(8,128)(2,1)} async-done(((bf16[192,4096]{1,0:T(8,128)(2,1)}), bf16[192,2048]{1,0:T(8,128)(2,1)}) %reduce-scatter.2.cloned.1.call-update) | async-done | bytes 786448 | tf_op jit(solution)/shard_map/reduce_scatter | solution.py:120
  419.0 2.2 select_convert_fusion
  (121 shorter events, 26.2 us)
Async XLA Ops:
  6.5 32.3 %all-gather.8.cloned.1.call-start = ((), (), s32[]{:S(2)}) async-start(), calls=%async_computation.1 | async-start | bytes 2359296 | tf_op jit(solution)/shard_map/all_gather | solution.py:84
  7.3 84.1 %all-gather.10.cloned.1.call-start = ((), (), s32[]{:S(2)}) async-start(), calls=%async_computation.2 | async-start | bytes 4456448 | tf_op jit(solution)/shard_map/all_gather | solution.py:90
  8.0 134.5 %all-gather.16.cloned.1.call-start = ((), (), s32[]{:S(2)}) async-start(), calls=%async_computation.5 | async-start | bytes 4456448 | tf_op jit(solution)/shard_map/all_gather | solution.py:91
  8.7 179.9 %all-gather.12.cloned.1.call-start = ((), (), s32[]{:S(2)}) async-start(), calls=%async_computation.3 | async-start | bytes 3342336 | tf_op jit(solution)/shard_map/all_gather | solution.py:108
  40.6 101.9 %copy-start.1 = (bf16[192,4096]{1,0:T(8,128)(2,1)S(1)}, bf16[192,4096]{1,0:T(8,128)(2,1)}, u32[]{:S(2)}) copy-start(bf16[192,4096]{1,0:T(8,128)(2,1)} %all-gather.8.cloned.1.call-done) | copy-start | bytes 4718596
  40.6 101.9 %copy-start.5 = (f32[4096]{0:T(1024)S(1)}, f32[4096]{0:T(1024)}, u32[]{:S(2)}) copy-start(f32[4096]{0:T(1024)} %param.11) | copy-start | bytes 49156
  95.8 52.0 %copy-start.6 = (u32[32]{0:T(128)S(1)}, u32[32]{0:T(128)}, u32[]{:S(2)}) copy-start(u32[32]{0:T(128)} %constant.95) | copy-start | bytes 388
  95.8 53.3 %copy-start.4 = (s32[192]{0:T(256)S(1)}, s32[192]{0:T(256)}, u32[]{:S(2)}) copy-start(s32[192]{0:T(256)} %param.10) | copy-start | bytes 2308
  95.8 139.1 %all-gather.18.cloned.1.call-start = ((), (), s32[]{:S(2)}) async-start(), calls=%async_computation.6 | async-start | bytes 3342336 | tf_op jit(solution)/shard_map/all_gather | solution.py:109
  146.4 163.2 %all-gather.14.cloned.1.call-start = ((), (), s32[]{:S(2)}) async-start(), calls=%async_computation.4 | async-start | bytes 8912896 | tf_op jit(solution)/shard_map/all_gather | solution.py:89
  147.0 241.1 %all-gather.20.cloned.1.call-start = ((), (), s32[]{:S(2)}) async-start(), calls=%async_computation.7 | async-start | bytes 8912896 | tf_op jit(solution)/shard_map/all_gather | solution.py:117
  147.8 271.3 %reduce-scatter.2.cloned.1.call-start = ((), (), s32[]{:S(2)}) async-start(), calls=%async_computation.8 | async-start | bytes 2359296 | tf_op jit(solution)/shard_map/reduce_scatter | solution.py:120
  320.3 1.2 copy-start
  320.3 1.3 copy-start.2
  322.8 0.9 copy-start.3
  328.1 1.2 copy-start
  328.1 1.3 copy-start.2
  330.6 0.9 copy-start.3
  335.8 1.2 copy-start
  335.8 1.3 copy-start.2
  338.3 0.9 copy-start.3
  343.5 1.2 copy-start
  343.5 1.3 copy-start.2
  346.0 0.9 copy-start.3
  351.3 1.2 copy-start
  351.3 1.3 copy-start.2
  353.8 0.9 copy-start.3
  359.1 1.2 copy-start
  359.1 1.3 copy-start.2
  361.6 0.9 copy-start.3
Sparse Core Ops, SparseCore 0:
  8.9 29.8 all-gather.7
  41.0 50.3 all-gather.9
  93.6 48.8 all-gather.15
  144.6 43.9 all-gather.11
  190.8 44.1 all-gather.17
  237.0 72.6 all-gather.13
  311.8 76.2 all-gather.19
  394.7 24.3 reduce-scatter.1
where the time goes:
time: 429 us; the launch traced here: 428 us
  waiting for transfers between devices  295 us (69%)
  matrix products  37.7 us (9%)
  local copies, waits for them, and re-layouts  34.3 us (8%)
  blocking collectives  32.5 us (8%)
  between operations  14.3 us (3%)
  other arithmetic  13.1 us (3%)
    all_gather x1, waiting for transfers between devices, body(): lax.all_gather(w_query, 'seq', axis=0, tiled=True)  69.2 us
    all_gather x1, waiting for transfers between devices, body(): lax.all_gather(w_key, 'seq', axis=0, tiled=True)  50.7 us
    all_gather x1, waiting for transfers between devices, body(): lax.all_gather(w_value, 'seq', axis=0, tiled=True)  46.6 us
    all_gather x1, waiting for transfers between devices, body(): lax.all_gather(values_local, 'seq', axis=0, tiled=True)  40.7 us
    unnamed x1, blocking collectives  32.5 us
    all_gather x1, waiting for transfers between devices, body(): gathered = lax.all_gather(hidden, 'tensor', axis=1, tiled=True)  30 us
    reduce_scatter x1, waiting for transfers between devices, body(): lax.psum_scatter(branch_terms.astype(jnp.bfloat16), 'tensor', scatter_dim...  24.5 us
    all_gather x1, waiting for transfers between devices, body(): lax.all_gather(w_out, 'seq', axis=1, tiled=True)  23.6 us
  transfers between devices with their start and end apart: 8, of which 8 were waited for; matrix products, arithmetic and copies ran while one was open for 16% of the time, Pallas kernels for 0%

commit v1 on v0

--- a/solution.py
+++ b/solution.py
@@ -81,7 +81,7 @@
 def body(hidden, depth, norm_gain, w_query, w_key, w_value, w_out):
     row_count = hidden.shape[0]
     my_index = lax.axis_index("seq")
-    gathered = lax.all_gather(hidden, "tensor", axis=1, tiled=True)
+    gathered = jnp.concatenate(lax.all_gather(hidden, axis_name="tensor"), 1)
     widened = gathered.astype(jnp.float32)
     inverse = lax.rsqrt(jnp.mean(widened * widened, axis=1, keepdims=True) + EPSILON)
     normed = (widened * inverse * norm_gain[None, :]).astype(jnp.bfloat16)

time: 429 us -> 429 us (level)
  local copies, waits for them, and re-layouts: 34.3 us -> 39.9 us
    all_gather x1, waiting for transfers between devices: 50.7 us -> 45.9 us  [body(): lax.all_gather(w_key, 'seq', axis=0, tiled=True)]
  transfers between devices with their start and end apart: 8 -> 8, of which waited for: 8 -> 8; matrix products, arithmetic and copies ran while one was open for 16% -> 18% of each run, Pallas kernels for 0% -> 0%
where the time goes in v1:
time: 429 us; the launch traced here: 428 us
  waiting for transfers between devices  291 us (68%)
  local copies, waits for them, and re-layouts  39.9 us (9%)
  matrix products  37.5 us (9%)
  blocking collectives  32.7 us (8%)
  between operations  14.3 us (3%)
  other arithmetic  12.3 us (3%)
    all_gather x1, waiting for transfers between devices, body(): lax.all_gather(w_query, 'seq', axis=0, tiled=True)  69.2 us
    all_gather x1, waiting for transfers between devices, body(): lax.all_gather(w_value, 'seq', axis=0, tiled=True)  47.2 us
    all_gather x1, waiting for transfers between devices, body(): lax.all_gather(w_key, 'seq', axis=0, tiled=True)  45.9 us
    all_gather x1, waiting for transfers between devices, body(): lax.all_gather(values_local, 'seq', axis=0, tiled=True)  40.5 us
    unnamed x1, blocking collectives  32.7 us
    all_gather x1, waiting for transfers between devices, body(): gathered = jnp.concatenate(lax.all_gather(hidden, axis_name='tensor'), 1)  30 us
    reduce_scatter x1, waiting for transfers between devices, body(): lax.psum_scatter(branch_terms.astype(jnp.bfloat16), 'tensor', scatter_dim...  24.5 us
    all_gather x1, waiting for transfers between devices, body(): lax.all_gather(w_out, 'seq', axis=1, tiled=True)  23.2 us
  transfers between devices with their start and end apart: 8, of which 8 were waited for; matrix products, arithmetic and copies ran while one was open for 18% of the time, Pallas kernels for 0%

profile of v1, /device:TPU:0, one launch (start us, length us, event | category | flops | bytes accessed | tf_op | source)
XLA Modules:
  0.0 428.1 jit_solution(12490174095723024744)
XLA Ops:
  8.8 30.0 %all-gather.21.cloned.1.call-done = bf16[384,2048]{1,0:T(8,128)(2,1)} async-done(((bf16[192,2048]{1,0:T(8,128)(2,1)}), bf16[384,2048]{1,0:T(8,128)(2,1)}) %all-gather.21.cloned.1.call-update) | async-done | bytes 1572880 | tf_op jit(solution)/shard_map/all_gather | solution.py:84
  38.8 3.1 copy.11
  41.9 2.7 copy.20
  45.5 45.9 %all-gather.9.cloned.1.call-done = bf16[4096,512]{1,0:T(8,128)(2,1)} async-done(((bf16[256,512]{1,0:T(8,128)(2,1)}), bf16[4096,512]{1,0:T(8,128)(2,1)}) %all-gather.9.cloned.1.call-update) | async-done | bytes 4194320 | tf_op jit(solution)/shard_map/all_gather | solution.py:90
  91.4 3.9 convolution_convert_fusion.3
  95.3 47.2 %all-gather.15.cloned.1.call-done = bf16[4096,512]{1,0:T(8,128)(2,1)} async-done(((bf16[256,512]{1,0:T(8,128)(2,1)}), bf16[4096,512]{1,0:T(8,128)(2,1)}) %all-gather.15.cloned.1.call-update) | async-done | bytes 4194320 | tf_op jit(solution)/shard_map/all_gather | solution.py:91
  142.5 3.8 convolution_convert_fusion.2
  149.4 32.7 %all-reduce = bf16[3072]{0:T(1024)(128)(2,1)S(1)} all-reduce(bf16[3072]{0:T(1024)(128)(2,1)S(1)} %dynamic-update-slice), channel_id=1, replica_groups=mesh['seq'=16,'tensor'=2] {'seq'}, use_global_device_ids=true, to_apply=%add | all-reduce | flops 3072 | bytes 12288
  182.1 6.7 %all-gather.11.cloned.1.call-done = bf16[3072,512]{1,0:T(8,128)(2,1)} async-done(((bf16[192,512]{1,0:T(8,128)(2,1)}), bf16[3072,512]{1,0:T(8,128)(2,1)}) %all-gather.11.cloned.1.call-update) | async-done | bytes 3145744 | tf_op jit(solution)/shard_map/all_gather | solution.py:108
  188.9 5.5 %reshape.135 = bf16[6,512,4,128]{3,2,1,0:T(4,128)(2,1)} reshape(bf16[3072,512]{1,0:T(8,128)(2,1)} %all-gather.11.cloned.1.call-done) | data formatting | bytes 6291456 | tf_op jit(solution)/shard_map/reshape | solution.py:54
  194.4 40.5 %all-gather.17.cloned.1.call-done = bf16[3072,512]{1,0:T(8,128)(2,1)} async-done(((bf16[192,512]{1,0:T(8,128)(2,1)}), bf16[3072,512]{1,0:T(8,128)(2,1)}) %all-gather.17.cloned.1.call-update) | async-done | bytes 3145744 | tf_op jit(solution)/shard_map/all_gather | solution.py:109
  234.9 5.5 %reshape.137 = bf16[6,512,4,128]{3,2,1,0:T(4,128)(2,1)} reshape(bf16[3072,512]{1,0:T(8,128)(2,1)} %all-gather.17.cloned.1.call-done) | data formatting | bytes 6291456 | tf_op jit(solution)/shard_map/reshape | solution.py:55
  240.5 69.2 %all-gather.13.cloned.1.call-done = bf16[4096,1024]{1,0:T(8,128)(2,1)} async-done(((bf16[256,1024]{1,0:T(8,128)(2,1)}), bf16[4096,1024]{1,0:T(8,128)(2,1)}) %all-gather.13.cloned.1.call-update) | async-done | bytes 8388624 | tf_op jit(solution)/shard_map/all_gather | solution.py:89
  309.6 5.2 %convolution_convert_fusion.1 = bf16[192,1024]{1,0:T(8,128)(2,1)S(1)} fusion(bf16[192,4096]{1,0:T(8,128)(2,1)S(1)} %multiply_convert_fusion, bf16[4096,1024]{1,0:T(8,128)(2,1)} %all-gather.13.cloned.1.call-done), kind=kOutput, calls=%fused_computation.39 | convolution fusion | flops 1610809344 | bytes 10354688 | tf_op jit(solution)/shard_map/dot_general | solution.py:94
  316.0 46.8 %while.17 = (s32[]{:T(128)}, f32[4,2,192]{2,1,0:T(2,128)S(1)}, f32[4,2,192]{2,1,0:T(2,128)S(1)}, f32[4,2,192,128]{3,2,1,0:T(8,128)}, bf16[6,512]{1,0:T(8,128)(2,...) while((s32[]{:T(128)}, f32[4,2,192]{2,1,0:T(2,128)S(1)}, ...), condition=%wide.region_4.5_spmd.clone, body=%wide.region_1.4_spmd.clone.sunk | while | flops 412303360 | bytes 23443692 | solution.py:59
  316.2 2.4 constant_dynamic-slice_fusion.4
  318.6 1.8 fusion.44
  324.0 2.4 constant_dynamic-slice_fusion.4
  326.4 1.8 fusion.44
  331.8 2.4 constant_dynamic-slice_fusion.4
  334.2 1.8 fusion.44
  339.6 2.4 constant_dynamic-slice_fusion.4
  341.9 1.8 fusion.44
  347.3 2.4 constant_dynamic-slice_fusion.4
  349.8 1.8 fusion.44
  355.2 2.4 constant_dynamic-slice_fusion.4
  357.6 1.8 fusion.44
  362.8 1.4 fusion.22
  364.9 23.2 %all-gather.19.cloned.1.call-done = bf16[1024,4096]{1,0:T(8,128)(2,1)} async-done(((bf16[1024,256]{1,0:T(8,128)(2,1)}), bf16[1024,4096]{1,0:T(8,128)(2,1)}) %all-gather.19.cloned.1.call-update) | async-done | bytes 8388624 | tf_op jit(solution)/shard_map/all_gather | solution.py:117
  388.1 6.4 %convolution_convert_fusion = bf16[192,4096]{1,0:T(8,128)(2,1)} fusion(bf16[192,1024]{1,0:T(8,128)(2,1)S(1)} %convert_element_type.63, bf16[1024,4096]{1,0:T(8,128)(2,1)} %all-gather.19.cloned.1.call-done), kind=kOutput, calls=%fused_computation.35 | convolution fusion | flops 1611399168 | bytes 10354688 | tf_op jit(solution)/shard_map/dot_general | solution.py:115
  394.5 24.5 %reduce-scatter.2.cloned.1.call-done = bf16[192,2048]{1,0:T(8,128)(2,1)} async-done(((bf16[192,4096]{1,0:T(8,128)(2,1)}), bf16[192,2048]{1,0:T(8,128)(2,1)}) %reduce-scatter.2.cloned.1.call-update) | async-done | bytes 786448 | tf_op jit(solution)/shard_map/reduce_scatter | solution.py:120
  419.0 2.2 select_convert_fusion
  (124 shorter events, 28.6 us)
Async XLA Ops:
  6.5 32.3 %all-gather.21.cloned.1.call-start = ((), (), s32[]{:S(2)}) async-start(), calls=%async_computation.8 | async-start | bytes 2359296 | tf_op jit(solution)/shard_map/all_gather | solution.py:84
  7.3 84.1 %all-gather.9.cloned.1.call-start = ((), (), s32[]{:S(2)}) async-start(), calls=%async_computation.1 | async-start | bytes 4456448 | tf_op jit(solution)/shard_map/all_gather | solution.py:90
  8.0 134.5 %all-gather.15.cloned.1.call-start = ((), (), s32[]{:S(2)}) async-start(), calls=%async_computation.4 | async-start | bytes 4456448 | tf_op jit(solution)/shard_map/all_gather | solution.py:91
  8.7 180.1 %all-gather.11.cloned.1.call-start = ((), (), s32[]{:S(2)}) async-start(), calls=%async_computation.2 | async-start | bytes 3342336 | tf_op jit(solution)/shard_map/all_gather | solution.py:108
  41.9 2.8 copy-start.1
  41.9 3.2 copy-start.4
  95.3 52.5 %copy-start.6 = (u32[32]{0:T(128)S(1)}, u32[32]{0:T(128)}, u32[]{:S(2)}) copy-start(u32[32]{0:T(128)} %constant.95) | copy-start | bytes 388
  95.3 53.8 %copy-start.5 = (s32[192]{0:T(256)S(1)}, s32[192]{0:T(256)}, u32[]{:S(2)}) copy-start(s32[192]{0:T(256)} %param.10) | copy-start | bytes 2308
  95.3 139.7 %all-gather.17.cloned.1.call-start = ((), (), s32[]{:S(2)}) async-start(), calls=%async_computation.5 | async-start | bytes 3342336 | tf_op jit(solution)/shard_map/all_gather | solution.py:109
  146.4 163.3 %all-gather.13.cloned.1.call-start = ((), (), s32[]{:S(2)}) async-start(), calls=%async_computation.3 | async-start | bytes 8912896 | tf_op jit(solution)/shard_map/all_gather | solution.py:89
  147.0 241.2 %all-gather.19.cloned.1.call-start = ((), (), s32[]{:S(2)}) async-start(), calls=%async_computation.6 | async-start | bytes 8912896 | tf_op jit(solution)/shard_map/all_gather | solution.py:117
  147.7 271.3 %reduce-scatter.2.cloned.1.call-start = ((), (), s32[]{:S(2)}) async-start(), calls=%async_computation.7 | async-start | bytes 2359296 | tf_op jit(solution)/shard_map/reduce_scatter | solution.py:120
  320.3 1.2 copy-start
  320.4 1.3 copy-start.2
  322.9 0.9 copy-start.3
  328.1 1.2 copy-start
  328.1 1.3 copy-start.2
  330.7 0.9 copy-start.3
  335.9 1.2 copy-start
  335.9 1.3 copy-start.2
  338.5 0.9 copy-start.3
  343.7 1.2 copy-start
  343.7 1.3 copy-start.2
  346.3 0.9 copy-start.3
  351.5 1.2 copy-start
  351.5 1.3 copy-start.2
  354.1 0.9 copy-start.3
  359.3 1.2 copy-start
  359.3 1.3 copy-start.2
  361.9 0.9 copy-start.3
Sparse Core Ops, SparseCore 0:
  8.9 29.8 all-gather.20
  41.0 50.3 all-gather.8
  93.6 48.8 all-gather.14
  144.6 44.1 all-gather.10
  191.0 43.8 all-gather.16
  237.0 72.6 all-gather.12
  311.8 76.2 all-gather.18
  394.7 24.3 reduce-scatter.1
